TPU v7x, 256 devices: a whole 4x4x8 slice. The times are simulated.
256 devices in a mesh: row: 32 (over x, z), col: 8 (over y, core).
Axes of the slice: x: 4, y: 4, z: 8, core: 2. Of those that a mesh axis runs over, the one named last changes fastest.
Arguments:
- momentum: float32 [5120, 13312], P('row', 'col')
- gradient: float32 [5120, 13312], P('row', 'col'), may hold values from -6 to 6
Outputs:
- new_momentum: float32 [5120, 13312], P('row', 'col')
- update: float32 [5120, 13312], P('row', 'col')
All inputs are finite; a program needn't handle non-finite values.
Results may differ from a plain program's by a relative error of at most 0.00073.
The roundings to bfloat16 on the way count: a program that leaves them out, or rounds other values in their place, can miss the bound.
Values may be sent and summed in bfloat16 or wider, within the bound.
A program may use at most 64 MiB of HBM per device.

v0:
```python
import functools
import jax
import jax.numpy as jnp
from jax import lax
from jax.sharding import Mesh
from jax.sharding import PartitionSpec as P

D = 5120
FF_WIN = 13312
ROW_COL = ("row_0", "row_1", "col_0", "col_1")
ROW = ("row_0", "row_1")
COL = ("col_0", "col_1")


def by_axis(array, axes):
    return functools.reduce(lax.psum, axes, array)


def gram_rows(left, right):
    return lax.dot_general(
        left, right, (((1,), (1,)), ((), ())), preferred_element_type=jnp.float32
    )


def shards(momentum, gradient):
    new_momentum = 0.95 * momentum + gradient
    squares = by_axis(jnp.sum(new_momentum * new_momentum), ROW_COL)
    normed = new_momentum / (jnp.sqrt(3.0 * squares / D) + 1e-07)
    rounded = normed.astype(jnp.bfloat16)
    gathered = lax.all_gather(rounded, ROW, axis=0, tiled=True)
    partial_value = gram_rows(rounded, gathered)
    gram = lax.psum(partial_value, COL)
    gram_rounded = gram.astype(jnp.bfloat16)
    product = jnp.dot(gram_rounded, gathered, preferred_element_type=jnp.float32)
    update = (1.5 * normed - 0.5 * product) * jnp.sqrt(jnp.float32(3 * FF_WIN))
    return (new_momentum, update)


def solution(mesh):
    torus = Mesh(mesh.devices.reshape(4, 8, 4, 2), ("row_0", "row_1", "col_0", "col_1"))
    return jax.shard_map(
        shards,
        mesh=torus,
        in_specs=(P(ROW, COL), P(ROW, COL)),
        out_specs=(P(ROW, COL), P(ROW, COL)),
        check_vma=False,
    )
```

profile of v0, /device:TPU:25, one launch (start us, length us, event | category | flops | bytes accessed | tf_op | source)
XLA Modules:
  0.0 273.7 jit_solution(8420792981213836205)
XLA Ops:
  7.2 0.0 all-gather.2.cloned.1.call-start
  7.2 2.4 multiply_reduce_fusion
  9.6 0.0 copy-start
  9.6 9.1 %psum.35 = f32[]{:T(128)} all-reduce(f32[]{:T(128)} %get-tuple-element.2), channel_id=1, replica_groups=mesh['row_0'=4,'row_1'=8,'col_0'=4,'col_1'=2] {'row_0'}, use_global_device_ids=true, to_apply=%region_1.0 | all-reduce | flops 1 | bytes 8 | tf_op jit(solution)/shard_map/psum | solution.py:16
  18.7 16.9 %psum.36 = f32[]{:T(128)} all-reduce(f32[]{:T(128)} %psum.35), channel_id=1, replica_groups=mesh['row_0'=4,'row_1'=8,'col_0'=4,'col_1'=2] {'row_1'}, use_global_device_ids=true, to_apply=%region_2.0 | all-reduce | flops 1 | bytes 8 | tf_op jit(solution)/shard_map/psum | solution.py:16
  35.6 6.4 %psum.37 = f32[]{:T(128)} all-reduce(f32[]{:T(128)} %psum.36), channel_id=1, replica_groups=mesh['row_0'=4,'row_1'=8,'col_0'=4,'col_1'=2] {'col_0'}, use_global_device_ids=true, to_apply=%region_3.0 | all-reduce | flops 1 | bytes 8 | tf_op jit(solution)/shard_map/psum | solution.py:16
  41.9 10.9 %psum.38 = f32[]{:T(128)} all-reduce(f32[]{:T(128)} %psum.37), channel_id=1, replica_groups=mesh['row_0'=4,'row_1'=8,'col_0'=4,'col_1'=2] {'col_1'}, use_global_device_ids=true, to_apply=%region_4.0 | all-reduce | flops 1 | bytes 8 | tf_op jit(solution)/shard_map/psum | solution.py:16
  53.5 0.9 fusion.3
  54.4 0.0 all-gather.2.cloned.1.call-update
  54.4 0.0 copy-done
  54.4 136.6 %all-gather.2.cloned.1.call-done = bf16[5120,1664]{1,0:T(8,128)(2,1)} async-done(((bf16[160,1664]{1,0:T(8,128)(2,1)}), bf16[5120,1664]{1,0:T(8,128)(2,1)}) %all-gather.2.cloned.1.call-update) | async-done | bytes 17039376 | tf_op jit(solution)/shard_map/all_gather | solution.py:30
  191.0 9.3 %fusion.4 = f32[160,5120]{1,0:T(8,128)S(1)} fusion(bf16[160,1664]{1,0:T(8,128)(2,1)} %fusion.3, bf16[5120,1664]{1,0:T(8,128)(2,1)} %all-gather.2.cloned.1.call-done), kind=kOutput, calls=%fused_computation.8 | convolution fusion | flops 2726297600 | bytes 20848640 | tf_op jit(solution)/shard_map/dot_general | solution.py:20
  200.3 55.8 %all-reduce.1 = bf16[160,5120]{1,0:T(8,128)(2,1)} all-reduce(f32[160,5120]{1,0:T(8,128)S(1)} %fusion.4), channel_id=1, replica_groups=mesh['row_0'=4,'row_1'=8,'col_0'=4,'col_1'=2] {'col_0','col_1'}, use_global_device_ids=true, to_apply=%region_5.0 | all-reduce | flops 819200 | bytes 4915200 | tf_op jit(solution)/shard_map/psum | solution.py:32
  256.1 10.8 %fusion.1 = f32[160,1664]{1,0:T(8,128)} fusion(bf16[5120,1664]{1,0:T(8,128)(2,1)} %all-gather.2.cloned.1.call-done, bf16[160,5120]{1,0:T(8,128)(2,1)} %all-reduce.1, f32[160,1664]{1,0:T(8,128)} %copy-done, f32[]{:T(128)S(6)} %add.17), kind=kOutput, calls=%fused_computation.2 | convolution fusion | flops 2727628800 | bytes 20807684 | tf_op jit(solution)/shard_map/dot_general | solution.py:34
Async XLA Ops:
  7.2 183.8 %all-gather.2.cloned.1.call-start = ((), (), s32[]{:S(2)}) async-start(), calls=%async_computation | async-start | bytes 17571840 | tf_op jit(solution)/shard_map/all_gather | solution.py:30
  9.6 44.8 %copy-start = (f32[160,1664]{1,0:T(8,128)}, f32[160,1664]{1,0:T(8,128)S(1)}, u32[]{:S(2)}) copy-start(f32[160,1664]{1,0:T(8,128)S(1)} %get-tuple-element.3) | copy-start | bytes 3194884
Sparse Core Ops, SparseCore 0:
  54.6 136.4 all-gather.1
where the time goes:
time: 274 us
  waiting for transfers between devices  137 us (50%)
  blocking collectives  99 us (36%)
  matrix products  20 us (7%)
  between operations  14.7 us (5%)
  other arithmetic  3.3 us (1%)
    all_gather x1, waiting for transfers between devices, shards(): gathered = lax.all_gather(rounded, ROW, axis=0, tiled=True)  137 us
    psum x1, blocking collectives, shards(): gram = lax.psum(partial_value, COL)  55.8 us
    psum x4, blocking collectives, by_axis(): return functools.reduce(lax.psum, axes, array)  43.2 us
    dot_general x1, matrix products, shards(): jnp.dot(gram_rounded, gathered, preferred_element_type=jnp.float32)  10.8 us
    dot_general x1, matrix products, gram_rows(): lax.dot_general(left, right, (((1,), (1,)), ((), ())), preferred_element_...  9.28 us
  transfers between devices with their start and end apart: 1, of which 1 were waited for; matrix products, arithmetic and copies ran while one was open for 0% of the time, Pallas kernels for 0%

commit v1 on v0

--- a/solution.py
+++ b/solution.py
@@ -10,6 +10,15 @@
 ROW_COL = ("row_0", "row_1", "col_0", "col_1")
 ROW = ("row_0", "row_1")
 COL = ("col_0", "col_1")
+
+
+def _work_rings(local_array, ax_name):
+    z = jax.lax.all_gather(local_array, ax_name)
+    v1 = jnp.sum(z, axis=0)
+    return v1
+
+
+keep_up_ports = functools.partial(_work_rings, ax_name=COL)
 
 
 def by_axis(array, axes):
@@ -29,7 +38,7 @@
     rounded = normed.astype(jnp.bfloat16)
     gathered = lax.all_gather(rounded, ROW, axis=0, tiled=True)
     partial_value = gram_rows(rounded, gathered)
-    gram = lax.psum(partial_value, COL)
+    gram = keep_up_ports(partial_value)
     gram_rounded = gram.astype(jnp.bfloat16)
     product = jnp.dot(gram_rounded, gathered, preferred_element_type=jnp.float32)
     update = (1.5 * normed - 0.5 * product) * jnp.sqrt(jnp.float32(3 * FF_WIN))

time: 274 us -> 358 us (1.31)
  waiting for transfers between devices: 137 us -> 261 us
  blocking collectives: 99 us -> 43.2 us
  other arithmetic: 3.3 us -> 13.4 us
    all_gather x0 -> x1, waiting for transfers between devices: none -> 124 us  [_work_rings(): z = jax.lax.all_gather(local_array, ax_name)]
    psum x1 -> x0, blocking collectives: 55.8 us -> none  [shards(): gram = lax.psum(partial_value, COL)]
    reduce_sum x0 -> x1, other arithmetic: none -> 10.1 us  [_work_rings(): v1 = jnp.sum(z, axis=0)]
    dot_general x1, matrix products: 9.28 us -> 13.3 us  [gram_rows(): lax.dot_general(left, right, (((1,), (1,)), ((), ())), preferred_element_...]
  transfers between devices with their start and end apart: 1 -> 2, of which waited for: 1 -> 2; matrix products, arithmetic and copies ran while one was open for 0% -> 0% of each run, Pallas kernels for 0% -> 0%
where the time goes in v1:
time: 358 us; the launch traced here: 356 us
  waiting for transfers between devices  261 us (73%)
  blocking collectives  43.2 us (12%)
  matrix products  23.3 us (7%)
  between operations  14.7 us (4%)
  other arithmetic  13.4 us (4%)
    all_gather x1, waiting for transfers between devices, shards(): gathered = lax.all_gather(rounded, ROW, axis=0, tiled=True)  137 us
    all_gather x1, waiting for transfers between devices, _work_rings(): z = jax.lax.all_gather(local_array, ax_name)  124 us
    psum x4, blocking collectives, by_axis(): return functools.reduce(lax.psum, axes, array)  43.2 us
    dot_general x1, matrix products, gram_rows(): lax.dot_general(left, right, (((1,), (1,)), ((), ())), preferred_element_...  13.3 us
    reduce_sum x1, other arithmetic, _work_rings(): v1 = jnp.sum(z, axis=0)  10.1 us
    dot_general x1, matrix products, shards(): jnp.dot(gram_rounded, gathered, preferred_element_type=jnp.float32)  10 us
  transfers between devices with their start and end apart: 2, of which 2 were waited for; matrix products, arithmetic and copies ran while one was open for 0% of the time, Pallas kernels for 0%

profile of v1, /device:TPU:25, one launch (start us, length us, event | category | flops | bytes accessed | tf_op | source)
XLA Modules:
  0.0 355.7 jit_solution(11252584361960266296)
XLA Ops:
  7.2 0.0 all-gather.4.cloned.1.call-start
  7.2 2.4 multiply_reduce_fusion
  9.6 0.0 copy-start
  9.6 9.1 %psum.28 = f32[]{:T(128)} all-reduce(f32[]{:T(128)} %get-tuple-element.2), channel_id=1, replica_groups=mesh['row_0'=4,'row_1'=8,'col_0'=4,'col_1'=2] {'row_0'}, use_global_device_ids=true, to_apply=%region_1.0 | all-reduce | flops 1 | bytes 8 | tf_op jit(solution)/shard_map/psum | solution.py:25
  18.7 16.9 %psum.29 = f32[]{:T(128)} all-reduce(f32[]{:T(128)} %psum.28), channel_id=1, replica_groups=mesh['row_0'=4,'row_1'=8,'col_0'=4,'col_1'=2] {'row_1'}, use_global_device_ids=true, to_apply=%region_2.0 | all-reduce | flops 1 | bytes 8 | tf_op jit(solution)/shard_map/psum | solution.py:25
  35.6 6.4 %psum.30 = f32[]{:T(128)} all-reduce(f32[]{:T(128)} %psum.29), channel_id=1, replica_groups=mesh['row_0'=4,'row_1'=8,'col_0'=4,'col_1'=2] {'col_0'}, use_global_device_ids=true, to_apply=%region_3.0 | all-reduce | flops 1 | bytes 8 | tf_op jit(solution)/shard_map/psum | solution.py:25
  41.9 10.9 %psum.31 = f32[]{:T(128)} all-reduce(f32[]{:T(128)} %psum.30), channel_id=1, replica_groups=mesh['row_0'=4,'row_1'=8,'col_0'=4,'col_1'=2] {'col_1'}, use_global_device_ids=true, to_apply=%region_4.0 | all-reduce | flops 1 | bytes 8 | tf_op jit(solution)/shard_map/psum | solution.py:25
  53.5 0.9 fusion.3
  54.4 0.0 all-gather.4.cloned.1.call-update
  54.4 0.0 all-gather.6.cloned.1.call-start
  54.5 136.6 %all-gather.4.cloned.1.call-done = bf16[5120,1664]{1,0:T(8,128)(2,1)} async-done(((bf16[160,1664]{1,0:T(8,128)(2,1)}), bf16[5120,1664]{1,0:T(8,128)(2,1)}) %all-gather.4.cloned.1.call-update) | async-done | bytes 17039376 | tf_op jit(solution)/shard_map/all_gather | solution.py:39
  191.0 13.3 %fusion.4 = f32[160,5120]{1,0:T(8,128)} fusion(bf16[160,1664]{1,0:T(8,128)(2,1)} %fusion.3, bf16[5120,1664]{1,0:T(8,128)(2,1)} %all-gather.4.cloned.1.call-done), kind=kOutput, calls=%fused_computation.8 | convolution fusion | flops 2726297600 | bytes 20848640 | tf_op jit(solution)/shard_map/dot_general | solution.py:29
  204.4 0.0 all-gather.6.cloned.1.call-update
  204.4 124.4 %all-gather.6.cloned.1.call-done = f32[1280,5120]{1,0:T(8,128)} async-done(((f32[160,5120]{1,0:T(8,128)}), f32[1280,5120]{1,0:T(8,128)}) %all-gather.6.cloned.1.call-update) | async-done | bytes 26214416 | tf_op jit(solution)/shard_map/all_gather | solution.py:16
  328.8 10.1 %reduce_sum.19 = bf16[160,5120]{1,0:T(8,128)(2,1)S(1)} reduce(f32[8,160,5120]{2,1,0:T(8,128)} %bitcast.5, f32[]{:T(128)} %constant.2.clone.1), dimensions={0}, to_apply=%region_5.0 | reduce | flops 5734400 | bytes 27852804 | tf_op jit(solution)/shard_map/reduce_sum | solution.py:17
  338.9 0.0 copy-done
  338.9 10.0 %fusion.1 = f32[160,1664]{1,0:T(8,128)} fusion(bf16[5120,1664]{1,0:T(8,128)(2,1)} %all-gather.4.cloned.1.call-done, bf16[160,5120]{1,0:T(8,128)(2,1)S(1)} %reduce_sum.19, f32[160,1664]{1,0:T(8,128)S(1)} %get-tuple-element.3, f32[]{:T(128)S(6)} %add.15), kind=kOutput, calls=%fused_computation.2 | convolution fusion | flops 2727628800 | bytes 20807684 | tf_op jit(solution)/shard_map/dot_general | solution.py:43
Async XLA Ops:
  7.2 183.9 %all-gather.4.cloned.1.call-start = ((), (), s32[]{:S(2)}) async-start(), calls=%async_computation | async-start | bytes 17571840 | tf_op jit(solution)/shard_map/all_gather | solution.py:39
  9.6 329.2 %copy-start = (f32[160,1664]{1,0:T(8,128)}, f32[160,1664]{1,0:T(8,128)S(1)}, u32[]{:S(2)}) copy-start(f32[160,1664]{1,0:T(8,128)S(1)} %get-tuple-element.3) | copy-start | bytes 3194884
  54.4 274.4 %all-gather.6.cloned.1.call-start = ((), (), s32[]{:S(2)}) async-start(), calls=%async_computation.1 | async-start | bytes 29491200 | tf_op jit(solution)/shard_map/all_gather | solution.py:16
Sparse Core Ops, SparseCore 0:
  54.6 136.4 all-gather.3
  204.5 124.2 all-gather.5
